TPU v7x, 512 devices: a whole 4x4x16 slice. The times are simulated.
512 devices in a mesh: feat: 32 (over x, y, core), rep: 16 (over z).
Axes of the slice: x: 4, y: 4, z: 16, core: 2. Of those that a mesh axis runs over, the one named last changes fastest.
Arguments:
- feats: bfloat16 [16, 8192, 1024], P('rep', None, 'feat'), may hold values from -6 to 6
- w_self: bfloat16 [1024, 256], P('feat'), may hold values from -0.1875 to 0.1875
- w_neigh: bfloat16 [1024, 256], P('feat'), may hold values from -0.1875 to 0.1875
- bias: float32 [256], replicated, may hold values from -3 to 3
- tile_weight: bfloat16 [16, 32, 3, 128, 128], P('rep'), may hold values from -0.375 to 0.375
- tile_src: int32 [16, 32, 3], P('rep'), may hold values from 0 to 63
- tile_count: int32 [16, 32], P('rep'), may hold values from 1 to 3
- owner_order: int32 [16, 32], P('rep'), may hold values from 0 to 31, each once within a row
- cotangent: bfloat16 [16, 4096, 256], P('rep', 'feat'), may hold values from -6 to 6
Outputs:
- hidden: bfloat16 [16, 4096, 256], P('rep', 'feat')
- grad_self: float32 [1024, 256], P('feat')
- grad_neigh: float32 [1024, 256], P('feat')
All inputs are finite; a program needn't handle non-finite values.
Results may differ from a plain program's by a relative error of at most 0.0055.
Values may be sent and summed in bfloat16 or wider, within the bound.
A program may use at most 64 MiB of HBM per device.

v0:
```python
import jax
import jax.numpy as jnp
from jax import lax
from jax.sharding import PartitionSpec as P


def transposed_product(left, right):
    return lax.dot_general(
        left, right, (((0,), (0,)), ((), ())), preferred_element_type=jnp.float32
    )


def body(feats, w_self, w_neigh, bias, tile_weight, tile_src, tile_count, owner_order, cotangent):
    block_rows = tile_weight.shape[3]
    tile_slots = tile_weight.shape[2]
    columns = feats.shape[2]
    by_block = feats[0].reshape(-1, block_rows, columns)
    in_use = jnp.arange(tile_slots)[None, :] < tile_count[0][:, None]
    masked = jnp.where(in_use[:, :, None, None], tile_weight[0], jnp.zeros((), jnp.bfloat16))
    sources = by_block[tile_src[0]]
    aggregate = jnp.einsum(
        "bkij,bkjc->bic", masked, sources, preferred_element_type=jnp.float32
    ).astype(jnp.bfloat16)
    target_rows = by_block[owner_order[0]].reshape(-1, columns)
    target_mean = aggregate[owner_order[0]].reshape(-1, columns)
    partial_sums = jnp.dot(target_rows, w_self, preferred_element_type=jnp.float32)
    partial_sums = partial_sums + jnp.dot(target_mean, w_neigh, preferred_element_type=jnp.float32)
    preact = lax.psum_scatter(partial_sums, "feat", scatter_dimension=0, tiled=True) + bias
    hidden = jax.nn.silu(preact).astype(jnp.bfloat16)
    squash = jax.nn.sigmoid(preact)
    output_grad = (
        cotangent[0].astype(jnp.float32) * squash * (1.0 + preact * (1.0 - squash))
    ).astype(jnp.bfloat16)
    pieces = lax.all_gather(output_grad, "feat", axis=0, tiled=True)
    grad_self = transposed_product(target_rows, pieces)
    grad_neigh = transposed_product(target_mean, pieces)
    grad_self, grad_neigh = lax.psum((grad_self, grad_neigh), "rep")
    return (hidden[None], grad_self, grad_neigh)


def solution(mesh):
    in_specs = (
        P("rep", None, "feat"),
        P("feat", None),
        P("feat", None),
        P(),
        P("rep", None, None, None, None),
        P("rep", None, None),
        P("rep", None),
        P("rep", None),
        P("rep", "feat", None),
    )
    out_specs = (P("rep", "feat", None), P("feat", None), P("feat", None))
    return jax.shard_map(body, mesh=mesh, in_specs=in_specs, out_specs=out_specs, check_vma=False)
```

profile of v0, /device:TPU:2, one launch (start us, length us, event | category | flops | bytes accessed | tf_op | source)
XLA Modules:
  0.0 341.3 jit_solution(3312335809542064258)
XLA Ops:
  7.2 0.0 copy-start
  7.2 0.0 reduce-scatter.2.cloned.1.call-start
  7.2 0.7 fusion.20
  7.9 0.7 compare_select_fusion
  8.6 0.7 iota_compare_fusion
  9.3 0.1 copy.18
  9.4 0.1 reshape.130
  9.5 1.2 copy.24
  10.7 0.3 copy.16
  11.0 0.6 gather_fusion
  11.6 0.7 gather_fusion.1
  12.4 3.2 fusion.4
  15.5 0.0 copy-start.2
  15.6 0.6 gather_fusion.2
  16.2 0.0 copy-done
  16.2 0.7 fusion.10
  16.9 0.0 copy-done.2
  16.9 2.7 convolution_add_fusion
  19.6 0.0 copy-start.1
  19.6 0.0 copy-start.3
  19.6 0.0 reduce-scatter.2.cloned.1.call-update
  19.7 0.0 all-gather.2.cloned.1.call-start
  19.7 109.6 %reduce-scatter.2.cloned.1.call-done = f32[128,256]{1,0:T(8,128)} async-done(((f32[4096,256]{1,0:T(8,128)}), f32[128,256]{1,0:T(8,128)}) %reduce-scatter.2.cloned.1.call-update) | async-done | bytes 131088 | tf_op jit(solution)/shard_map/reduce_scatter | solution.py:28
  129.4 0.0 copy-done.1
  129.4 0.0 copy-done.3
  129.4 1.6 fusion.17
  131.0 0.0 all-gather.2.cloned.1.call-update
  131.0 0.0 all-reduce.3.cloned.1.call-start
  131.0 59.8 %all-gather.2.cloned.1.call-done = bf16[4096,256]{1,0:T(8,128)(2,1)} async-done(((bf16[128,256]{1,0:T(8,128)(2,1)}), bf16[4096,256]{1,0:T(8,128)(2,1)}) %all-gather.2.cloned.1.call-update) | async-done | bytes 2097168 | tf_op jit(solution)/shard_map/all_gather | solution.py:34
  190.8 2.7 fusion.5
  193.5 2.7 fusion.8
  196.2 0.0 all-reduce.3.cloned.1.call-update
  196.2 135.8 %all-reduce.3.cloned.1.call-done = (f32[32,256]{1,0:T(8,128)}, f32[32,256]{1,0:T(8,128)}) async-done(((f32[32,256]{1,0:T(8,128)}, f32[32,256]{1,0:T(8,128)}), (f32[32,256]{1,0:T(8,128)}, f32[32,256]{1,0:T(8,128)})) %all-reduce.3.cloned.1.call-update) | async-done | bytes 65552 | tf_op jit(solution)/shard_map/psum | solution.py:37
  332.0 1.4 copy.43
  333.4 1.4 copy.44
  (2 shorter events, 0.0 us)
Async XLA Ops:
  7.2 9.0 %copy-start = (bf16[32,256]{1,0:T(8,128)(2,1)S(1)}, bf16[32,256]{1,0:T(8,128)(2,1)}, u32[]{:S(2)}) copy-start(bf16[32,256]{1,0:T(8,128)(2,1)} %param.10) | copy-start | bytes 49156
  7.2 122.2 %reduce-scatter.2.cloned.1.call-start = ((), (), s32[]{:S(2)}) async-start(), calls=%async_computation.1 | async-start | bytes 4325376 | tf_op jit(solution)/shard_map/reduce_scatter | solution.py:28
  15.5 1.4 copy-start.2
  19.6 109.7 %copy-start.1 = (bf16[1,128,256]{2,1,0:T(8,128)(2,1)S(1)}, bf16[1,128,256]{2,1,0:T(8,128)(2,1)}, u32[]{:S(2)}) copy-start(bf16[1,128,256]{2,1,0:T(8,128)(2,1)} %param.17) | copy-start | bytes 196612
  19.6 109.7 %copy-start.3 = (f32[256]{0:T(256)S(1)}, f32[256]{0:T(256)}, u32[]{:S(2)}) copy-start(f32[256]{0:T(256)} %param.12) | copy-start | bytes 3076
  19.7 171.2 %all-gather.2.cloned.1.call-start = ((), (), s32[]{:S(2)}) async-start(), calls=%async_computation.2 | async-start | bytes 2162688 | tf_op jit(solution)/shard_map/all_gather | solution.py:34
  131.0 201.0 %all-reduce.3.cloned.1.call-start = ((), (), s32[]{:S(2)}) async-start(), calls=%async_computation.3 | async-start | bytes 131072 | tf_op jit(solution)/shard_map/psum | solution.py:37
Sparse Core Ops, SparseCore 0:
  19.8 109.5 reduce-scatter.1
  132.5 58.2 all-gather.1
  196.3 135.6 all-reduce.2
where the time goes:
time: 342 us; the launch traced here: 341 us
  waiting for transfers between devices  305 us (89%)
  between operations  13.8 us (4%)
  matrix products  11.9 us (3%)
  local copies, waits for them, and re-layouts  6.39 us (2%)
  other arithmetic  3.69 us (1%)
    psum x1, waiting for transfers between devices, body(): grad_self, grad_neigh = lax.psum((grad_self, grad_neigh), 'rep')  136 us
    reduce_scatter x1, waiting for transfers between devices, body(): lax.psum_scatter(partial_sums, 'feat', scatter_dimension=0, tiled=True)  110 us
    all_gather x1, waiting for transfers between devices, body(): pieces = lax.all_gather(output_grad, 'feat', axis=0, tiled=True)  59.8 us
  transfers between devices with their start and end apart: 3, of which 3 were waited for; matrix products, arithmetic and copies ran while one was open for 0% of the time, Pallas kernels for 0%

commit v1 on v0

--- a/solution.py
+++ b/solution.py
@@ -31,7 +31,10 @@
     output_grad = (
         cotangent[0].astype(jnp.float32) * squash * (1.0 + preact * (1.0 - squash))
     ).astype(jnp.bfloat16)
-    pieces = lax.all_gather(output_grad, "feat", axis=0, tiled=True)
+    devices = lax.axis_size("feat")
+    shards = jnp.stack([output_grad for _ in range(devices)])
+    shards = lax.all_to_all(shards, "feat", split_axis=0, concat_axis=0)
+    pieces = jnp.concatenate(shards, axis=0)
     grad_self = transposed_product(target_rows, pieces)
     grad_neigh = transposed_product(target_mean, pieces)
     grad_self, grad_neigh = lax.psum((grad_self, grad_neigh), "rep")

time: 342 us -> 311 us (0.909)
  waiting for transfers between devices: 305 us -> 246 us
  blocking collectives: 0 us -> 31.3 us
    all_gather x1 -> x0, waiting for transfers between devices: 59.8 us -> none  [body(): pieces = lax.all_gather(output_grad, 'feat', axis=0, tiled=True)]
    all_to_all x0 -> x1, blocking collectives: none -> 31.3 us  [body(): shards = lax.all_to_all(shards, 'feat', split_axis=0, concat_axis=0)]
  transfers between devices with their start and end apart: 3 -> 2, of which waited for: 3 -> 2; matrix products, arithmetic and copies ran while one was open for 0% -> 0% of each run, Pallas kernels for 0% -> 0%
where the time goes in v1:
time: 311 us
  waiting for transfers between devices  246 us (79%)
  blocking collectives  31.3 us (10%)
  between operations  14.1 us (5%)
  matrix products  8.77 us (3%)
  local copies, waits for them, and re-layouts  6.62 us (2%)
  other arithmetic  3.68 us (1%)
    psum x1, waiting for transfers between devices, body(): grad_self, grad_neigh = lax.psum((grad_self, grad_neigh), 'rep')  136 us
    reduce_scatter x1, waiting for transfers between devices, body(): lax.psum_scatter(partial_sums, 'feat', scatter_dimension=0, tiled=True)  110 us
    all_to_all x1, blocking collectives, body(): shards = lax.all_to_all(shards, 'feat', split_axis=0, concat_axis=0)  31.3 us
  transfers between devices with their start and end apart: 2, of which 2 were waited for; matrix products, arithmetic and copies ran while one was open for 0% of the time, Pallas kernels for 0%

profile of v1, /device:TPU:2, one launch (start us, length us, event | category | flops | bytes accessed | tf_op | source)
XLA Modules:
  0.0 310.6 jit_solution(13807582159321670160)
XLA Ops:
  7.2 0.0 copy-start
  7.2 0.0 reduce-scatter.2.cloned.1.call-start
  7.2 0.7 fusion.14
  7.9 0.7 compare_select_fusion
  8.6 0.7 iota_compare_fusion
  9.3 0.1 copy.19
  9.4 0.1 reshape.133
  9.5 1.2 copy.25
  10.7 0.3 copy.17
  11.0 0.6 gather_fusion
  11.6 0.7 gather_fusion.1
  12.4 3.2 %fusion.4 = bf16[32,128,32]{1,2,0:T(8,128)(2,1)S(1)} fusion(bf16[32,3,128,32]{2,3,1,0:T(8,128)(2,1)S(1)} %bitcast.60, bf16[1,32,3,128,128]{4,3,2,1,0:T(8,128)(2,1)} %param.13, pred[32,3]{1,0:T(8,128)(4,1)S(1)} %iota_compare_fusion), kind=kOutput, calls=%fused_computation.9 | convolution fusion | flops 102367232 | bytes 4194400 | tf_op jit(solution)/shard_map/bkij,bkjc->bic/dot_general | solution.py:21
  15.5 0.0 copy-start.2
  15.6 0.6 gather_fusion.2
  16.2 0.0 copy-done
  16.2 0.7 fusion.7
  16.9 0.0 copy-done.2
  16.9 2.7 convolution_add_fusion
  19.6 0.0 copy-start.1
  19.6 0.0 copy-start.3
  19.6 0.0 reduce-scatter.2.cloned.1.call-update
  19.7 0.0 all-reduce.3.cloned.1.call-start
  19.7 109.6 %reduce-scatter.2.cloned.1.call-done = f32[128,256]{1,0:T(8,128)} async-done(((f32[4096,256]{1,0:T(8,128)}), f32[128,256]{1,0:T(8,128)}) %reduce-scatter.2.cloned.1.call-update) | async-done | bytes 131088 | tf_op jit(solution)/shard_map/reduce_scatter | solution.py:28
  129.3 0.0 copy-done.1
  129.4 0.0 copy-done.3
  129.4 1.6 fusion.11
  130.9 0.2 stack.2
  131.2 31.3 %all_to_all.5 = bf16[32,128,256]{2,1,0:T(8,128)(2,1)S(1)} all-to-all(bf16[32,128,256]{2,1,0:T(8,128)(2,1)S(1)} %stack.2), channel_id=1, replica_groups=mesh['feat'=32,'rep'=16] {'feat'}, dimensions={0} | all-to-all | bytes 4194304 | tf_op jit(solution)/shard_map/all_to_all | solution.py:36
  162.5 1.1 convolution_bitcast_fusion
  163.6 1.1 convolution_bitcast_fusion.1
  164.7 0.0 all-reduce.3.cloned.1.call-update
  164.7 136.4 %all-reduce.3.cloned.1.call-done = (f32[32,256]{1,0:T(8,128)}, f32[32,256]{1,0:T(8,128)}) async-done(((f32[32,256]{1,0:T(8,128)}, f32[32,256]{1,0:T(8,128)}), (f32[32,256]{1,0:T(8,128)}, f32[32,256]{1,0:T(8,128)})) %all-reduce.3.cloned.1.call-update) | async-done | bytes 65552 | tf_op jit(solution)/shard_map/psum | solution.py:40
  301.0 1.4 copy.36
  302.4 1.4 copy.37
  (2 shorter events, 0.0 us)
Async XLA Ops:
  7.2 9.0 %copy-start = (bf16[32,256]{1,0:T(8,128)(2,1)S(1)}, bf16[32,256]{1,0:T(8,128)(2,1)}, u32[]{:S(2)}) copy-start(bf16[32,256]{1,0:T(8,128)(2,1)} %param.10) | copy-start | bytes 49156
  7.2 122.2 %reduce-scatter.2.cloned.1.call-start = ((), (), s32[]{:S(2)}) async-start(), calls=%async_computation.2 | async-start | bytes 4325376 | tf_op jit(solution)/shard_map/reduce_scatter | solution.py:28
  15.5 1.4 copy-start.2
  19.6 109.7 %copy-start.1 = (bf16[1,128,256]{2,1,0:T(8,128)(2,1)S(1)}, bf16[1,128,256]{2,1,0:T(8,128)(2,1)}, u32[]{:S(2)}) copy-start(bf16[1,128,256]{2,1,0:T(8,128)(2,1)} %param.17) | copy-start | bytes 196612
  19.6 109.7 %copy-start.3 = (f32[256]{0:T(256)S(1)}, f32[256]{0:T(256)}, u32[]{:S(2)}) copy-start(f32[256]{0:T(256)} %param.12) | copy-start | bytes 3076
  19.7 281.4 %all-reduce.3.cloned.1.call-start = ((), (), s32[]{:S(2)}) async-start(), calls=%async_computation.3 | async-start | bytes 131072 | tf_op jit(solution)/shard_map/psum | solution.py:40
Sparse Core Ops, SparseCore 0:
  19.8 109.5 reduce-scatter.1
  164.8 136.1 all-reduce.2
